TPU v7x, 256 devices: a whole 4x4x8 slice. The times are simulated.
256 devices in a mesh: client: 32 (over z_lo, y, core), mp: 8 (over x, z_hi).
Axes of the slice: x: 4, y: 4, z: 8 (z_hi: 2, z_lo: 4; z = z_hi * 4 + z_lo), core: 2. Of those that a mesh axis runs over, the one named last changes fastest.
Arguments:
- hidden: bfloat16 [32, 4, 128, 7168], P('client', None, None, 'mp'), may hold values from -6 to 6
- weight: bfloat16 [32, 7168, 2048], P('client', 'mp'), may hold values from -0.0625 to 0.0625
- target: bfloat16 [32, 4, 128, 2048], P('client', None, 'mp'), may hold values from -6 to 6
- router_prob: float32 [32, 4, 128], P('client', None, 'mp'), may hold values from 0.2 to 1
- routes: int32 [32, 4, 128, 2], P('client', None, 'mp'), may hold values from 0 to 7, all different within a row
- assign: int32 [32, 1], replicated, may hold values from 0 to 3
Outputs:
- merged_weight: bfloat16 [32, 7168, 2048], P('client', 'mp')
Inputs may be any that keep to these rules, and one draw needn't show every extreme that they name: `routes`: each token names two different experts; the given weights are those of expert 0. `assign`: every cluster has at least one client.
All inputs are finite; a program needn't handle non-finite values.
Results may differ from a plain program's by a relative error of at most 0.0044.
The roundings to bfloat16 on the way count: a program that leaves them out, or rounds other values in their place, can miss the bound.
Values may be sent and summed in bfloat16 or wider, within the bound.
A program may use at most 128 MiB of HBM per device.

v0:
```python
import jax
import jax.numpy as jnp
from jax import lax
from jax.sharding import PartitionSpec as P

D = 2048
FFW = 7168
NB = 4
CLUSTERS = 4
EPS = 1e-06
FLOOR = 0.1


def body(hidden, weight, target, router_prob, routes, assign):
    local_weight = weight[0]
    fisher = jnp.zeros(local_weight.shape, jnp.float32)
    for batch in range(NB):
        batch_hidden = hidden[0, batch]
        outputs = lax.psum_scatter(
            jnp.dot(batch_hidden, local_weight, preferred_element_type=jnp.float32),
            "mp",
            scatter_dimension=0,
            tiled=True,
        )
        token_weight = jnp.where(
            jnp.any(routes[0, batch] == 0, axis=-1), router_prob[0, batch], 0.0
        )
        grad_out = (
            token_weight[:, None] * (outputs - target[0, batch].astype(jnp.float32))
        ).astype(jnp.bfloat16)
        grad = lax.dot_general(
            batch_hidden,
            lax.all_gather(grad_out, "mp", axis=0, tiled=True),
            (((0,), (0,)), ((), ())),
            preferred_element_type=jnp.float32,
        )
        fisher = fisher + grad * grad
    total_fisher = lax.psum(jnp.sum(fisher), "mp")
    mean_fisher = total_fisher / (FFW * D)
    a_weight = (fisher / (mean_fisher + EPS) + FLOOR).astype(jnp.bfloat16)
    got_a, got_w = (
        lax.all_to_all(a_weight[None], "client", split_axis=1, concat_axis=0, tiled=True),
        lax.all_to_all(local_weight[None], "client", split_axis=1, concat_axis=0, tiled=True),
    )
    member_table = (assign[:, 0][:, None] == jnp.arange(CLUSTERS)[None, :]).astype(jnp.float32)
    a_float = got_a.astype(jnp.float32)
    weighted = a_float * got_w.astype(jnp.float32)
    num_part = jnp.einsum("sk,srd->krd", member_table, weighted, precision=lax.Precision.HIGHEST)
    den_part = jnp.einsum("sk,srd->krd", member_table, a_float, precision=lax.Precision.HIGHEST)
    merged = (num_part / den_part).astype(jnp.bfloat16)
    own_cluster = lax.dynamic_index_in_dim(
        assign[:, 0], lax.axis_index("client"), 0, keepdims=False
    )
    every_cluster = lax.all_gather(merged, "client", axis=1, tiled=True)
    result = lax.dynamic_index_in_dim(every_cluster, own_cluster, 0, keepdims=True)
    return result


def solution(mesh):
    placed = (
        P("client", None, None, "mp"),
        P("client", "mp", None),
        P("client", None, "mp", None),
        P("client", None, "mp"),
        P("client", None, "mp", None),
        P(),
    )
    return jax.shard_map(
        body, mesh=mesh, in_specs=placed, out_specs=P("client", "mp", None), check_vma=False
    )
```

profile of v0, /device:TPU:1, one launch (start us, length us, event | category | flops | bytes accessed | tf_op | source)
XLA Modules:
  0.0 917.2 jit_solution(14706498457414140986)
XLA Ops:
  6.5 0.0 copy-start.1
  6.5 0.0 reduce-scatter.11.cloned.1.call-start
  6.5 3.9 fusion.2
  10.5 0.0 reduce-scatter.11.cloned.1.call-update
  10.5 0.0 reduce-scatter.5.cloned.1.call-start
  10.5 3.9 fusion.8
  14.4 0.0 reduce-scatter.5.cloned.1.call-update
  14.5 0.0 reduce-scatter.7.cloned.1.call-start
  14.5 0.0 copy-done.1
  14.5 3.8 fusion.6
  18.3 0.0 reduce-scatter.7.cloned.1.call-update
  18.3 7.8 copy.31
  26.1 0.6 broadcast.41
  26.7 23.7 %reduce.10 = bf16[896,2048]{1,0:T(8,128)(2,1)} reduce(bf16[896,1,2048]{2,1,0:T(2,128)(2,1)} %bitcast.73, bf16[]{:T(256)} %broadcast.41), dimensions={1}, to_apply=%bitcast.72.reduce_sub_computation | reduce | bytes 7340034
  50.3 8.7 reshape.64
  59.1 0.0 copy-start.3
  59.1 0.0 copy-start.5
  59.1 10.4 %all-to-all-start.1 = ((bf16[32,2,28672]{2,1,0:T(2,128)(2,1)}), bf16[32,2,28672]{2,1,0:T(2,128)(2,1)}, u32[]{:S(2)}, u32[]{:S(2)}) async-start(bf16[32,2,28672]{2,1,0:T(2,128)(2,1)} %reshape.64), calls=%async_computation.5 | async-start | bytes 7340032 | tf_op jit(solution)/shard_map/all_to_all | solution.py:43
  69.4 0.0 reduce-scatter.9.cloned.1.call-start
  69.5 3.7 fusion.4
  73.2 0.0 reduce-scatter.9.cloned.1.call-update
  73.3 0.0 copy-done.3
  73.3 0.0 copy-done.5
  73.3 27.6 %reduce-scatter.11.cloned.1.call-done = f32[16,2048]{1,0:T(8,128)} async-done(((f32[128,2048]{1,0:T(8,128)}), f32[16,2048]{1,0:T(8,128)}) %reduce-scatter.11.cloned.1.call-update) | async-done | bytes 131088 | tf_op jit(solution)/shard_map/reduce_scatter | solution.py:19
  100.9 95.0 %reduce-scatter.5.cloned.1.call-done = f32[16,2048]{1,0:T(8,128)} async-done(((f32[128,2048]{1,0:T(8,128)}), f32[16,2048]{1,0:T(8,128)}) %reduce-scatter.5.cloned.1.call-update) | async-done | bytes 131088 | tf_op jit(solution)/shard_map/reduce_scatter | solution.py:19
  195.9 86.6 %reduce-scatter.7.cloned.1.call-done = f32[16,2048]{1,0:T(8,128)} async-done(((f32[128,2048]{1,0:T(8,128)}), f32[16,2048]{1,0:T(8,128)}) %reduce-scatter.7.cloned.1.call-update) | async-done | bytes 131088 | tf_op jit(solution)/shard_map/reduce_scatter | solution.py:19
  282.5 87.1 %reduce-scatter.9.cloned.1.call-done = f32[16,2048]{1,0:T(8,128)} async-done(((f32[128,2048]{1,0:T(8,128)}), f32[16,2048]{1,0:T(8,128)}) %reduce-scatter.9.cloned.1.call-update) | async-done | bytes 131088 | tf_op jit(solution)/shard_map/reduce_scatter | solution.py:19
  369.7 0.0 copy-done.2
  369.7 1.2 fusion.39
  370.9 41.3 %all_gather.17 = bf16[128,2048]{1,0:T(8,128)(2,1)S(1)} all-gather(bf16[16,2048]{1,0:T(8,128)(2,1)S(1)} %get-tuple-element.12), channel_id=1, replica_groups=mesh['client'=32,'mp'=8] {'mp'}, dimensions={0}, use_global_device_ids=true | all-gather | bytes 589824 | tf_op jit(solution)/shard_map/all_gather | solution.py:33
  412.1 42.5 %all_gather.16 = bf16[128,2048]{1,0:T(8,128)(2,1)S(1)} all-gather(bf16[16,2048]{1,0:T(8,128)(2,1)S(1)} %get-tuple-element.10), channel_id=1, replica_groups=mesh['client'=32,'mp'=8] {'mp'}, dimensions={0}, use_global_device_ids=true | all-gather | bytes 589824 | tf_op jit(solution)/shard_map/all_gather | solution.py:33
  454.6 42.9 %all_gather.15 = bf16[128,2048]{1,0:T(8,128)(2,1)S(1)} all-gather(bf16[16,2048]{1,0:T(8,128)(2,1)S(1)} %get-tuple-element.11), channel_id=1, replica_groups=mesh['client'=32,'mp'=8] {'mp'}, dimensions={0}, use_global_device_ids=true | all-gather | bytes 589824 | tf_op jit(solution)/shard_map/all_gather | solution.py:33
  497.5 41.5 %all_gather.18 = bf16[128,2048]{1,0:T(8,128)(2,1)S(1)} all-gather(bf16[16,2048]{1,0:T(8,128)(2,1)S(1)} %get-tuple-element.9), channel_id=1, replica_groups=mesh['client'=32,'mp'=8] {'mp'}, dimensions={0}, use_global_device_ids=true | all-gather | bytes 589824 | tf_op jit(solution)/shard_map/all_gather | solution.py:33
  539.0 1.1 fusion.21
  540.2 1.1 fusion.24
  541.3 1.1 fusion.27
  542.5 4.9 fusion.51
  547.3 21.0 %psum.7 = f32[]{:T(128)} all-reduce(f32[]{:T(128)} %get-tuple-element.17), channel_id=1, replica_groups=mesh['client'=32,'mp'=8] {'mp'}, use_global_device_ids=true, to_apply=%region_9.10 | all-reduce | flops 1 | bytes 8 | tf_op jit(solution)/shard_map/psum | solution.py:38
  569.0 5.7 fusion.12
  574.7 18.1 %copy.15 = bf16[1,896,2048]{2,0,1:T(2,128)(2,1)} copy(bf16[1,896,2048]{1,2,0:T(8,128)(2,1)} %fusion.12) | data formatting | bytes 7340032 | tf_op jit(solution)/shard_map/broadcast_in_dim | solution.py:42
  592.8 23.7 %reduce.9 = bf16[896,2048]{1,0:T(8,128)(2,1)} reduce(bf16[896,1,2048]{2,1,0:T(2,128)(2,1)} %bitcast.74, bf16[]{:T(256)} %broadcast.41), dimensions={1}, to_apply=%bitcast.59.reduce_sub_computation | reduce | bytes 7340034
  616.5 8.7 reshape.62
  625.2 0.0 all-to-all-done.1
  625.2 38.2 %all-to-all-start = ((bf16[32,2,28672]{2,1,0:T(2,128)(2,1)}), bf16[32,2,28672]{2,1,0:T(2,128)(2,1)}, u32[]{:S(2)}, u32[]{:S(2)}) async-start(bf16[32,2,28672]{2,1,0:T(2,128)(2,1)} %reshape.62), calls=%async_computation.4 | async-start | bytes 7340032 | tf_op jit(solution)/shard_map/all_to_all | solution.py:42
  663.4 0.0 all-gather.2.cloned.1.call-start
  663.4 19.3 %reshape.65 = bf16[896,1,2048]{2,1,0:T(2,128)(2,1)} reshape(bf16[32,2,28672]{2,1,0:T(2,128)(2,1)} %all-to-all-done.1) | data formatting | bytes 7340032
  682.7 24.4 %convert_reduce_fusion = f32[896,2048]{1,0:T(8,128)} fusion(bf16[896,1,2048]{2,1,0:T(2,128)(2,1)} %reshape.65), kind=kLoop, calls=%fused_computation.4 | loop fusion | flops 1835008 | bytes 11010048 | tf_op jit(solution)/shard_map/convert_element_type | solution.py:47
  707.1 8.0 reshape.58
  715.1 30.2 %all-to-all-done = bf16[32,2,28672]{2,1,0:T(2,128)(2,1)} async-done(((bf16[32,2,28672]{2,1,0:T(2,128)(2,1)}), bf16[32,2,28672]{2,1,0:T(2,128)(2,1)}, u32[]{:S(2)}, u32[]{:S(2)}) %all-to-all-start) | async-done | bytes 3670048 | tf_op jit(solution)/shard_map/all_to_all | solution.py:42
  745.3 19.3 %reshape.63 = bf16[896,1,2048]{2,1,0:T(2,128)(2,1)} reshape(bf16[32,2,28672]{2,1,0:T(2,128)(2,1)} %all-to-all-done) | data formatting | bytes 7340032
  764.6 23.6 %bitcast_reduce_fusion = bf16[896,2048]{1,0:T(8,128)(2,1)} fusion(bf16[896,1,2048]{2,1,0:T(2,128)(2,1)} %reshape.63), kind=kLoop, calls=%fused_computation.65 | loop fusion | bytes 7340032 | tf_op jit(solution)/shard_map/all_to_all | solution.py:42
  788.2 5.9 all_to_all.7
  794.1 0.0 copy-start
  794.1 0.0 copy-start.4
  794.1 6.0 convert_multiply_fusion
  800.1 0.0 copy-done
  800.1 0.0 copy-done.4
  800.2 4.0 fusion.10
  804.2 7.7 fusion.16
  811.9 0.0 all-gather.2.cloned.1.call-update
  811.9 0.6 constant_dynamic-slice_fusion.1
  814.5 82.3 %all-gather.2.cloned.1.call-done = bf16[4,896,2048]{2,0,1:T(4,128)(2,1)} async-done(((bf16[4,28,2048]{2,0,1:T(4,128)(2,1)}), bf16[4,896,2048]{2,0,1:T(4,128)(2,1)}) %all-gather.2.cloned.1.call-update) | async-done | bytes 14680080 | tf_op jit(solution)/shard_map/all_gather | solution.py:54
  896.8 9.3 %constant_dynamic-slice_fusion = bf16[1,896,2048]{2,0,1:T(2,128)(2,1)S(1)} fusion(bf16[4,896,2048]{2,0,1:T(4,128)(2,1)} %all-gather.2.cloned.1.call-done, s32[]{:T(128)S(6)} %select_n.42), kind=kLoop, calls=%fused_computation.62 | loop fusion | bytes 7340036 | tf_op jit(solution)/shard_map/jit(dynamic_index_in_dim)/dynamic_slice | solution.py:55
  906.1 4.1 copy.19
  (3 shorter events, 0.0 us)
Async XLA Ops:
  6.5 8.0 copy-start.1
  6.5 94.4 %reduce-scatter.11.cloned.1.call-start = ((), (), s32[]{:S(2)}) async-start(), calls=%async_computation.9 | async-start | bytes 1179648 | tf_op jit(solution)/shard_map/reduce_scatter | solution.py:19
  10.5 185.4 %reduce-scatter.5.cloned.1.call-start = ((), (), s32[]{:S(2)}) async-start(), calls=%async_computation.6 | async-start | bytes 1179648 | tf_op jit(solution)/shard_map/reduce_scatter | solution.py:19
  14.5 268.1 %reduce-scatter.7.cloned.1.call-start = ((), (), s32[]{:S(2)}) async-start(), calls=%async_computation.7 | async-start | bytes 1179648 | tf_op jit(solution)/shard_map/reduce_scatter | solution.py:19
  59.1 14.2 %copy-start.3 = (s32[1,4,16,2]{2,3,1,0:T(2,128)S(1)}, s32[1,4,16,2]{2,3,1,0:T(2,128)}, u32[]{:S(2)}) copy-start(s32[1,4,16,2]{2,3,1,0:T(2,128)} %param.10) | copy-start | bytes 1540
  59.1 14.2 %copy-start.5 = (f32[1,4,16]{2,1,0:T(4,128)S(1)}, f32[1,4,16]{2,1,0:T(4,128)}, u32[]{:S(2)}) copy-start(f32[1,4,16]{2,1,0:T(4,128)} %param.9) | copy-start | bytes 772
  59.1 310.6 %copy-start.2 = (bf16[1,4,16,2048]{3,2,1,0:T(8,128)(2,1)S(1)}, bf16[1,4,16,2048]{3,2,1,0:T(8,128)(2,1)}, u32[]{:S(2)}) copy-start(bf16[1,4,16,2048]{3,2,1,0:T(8,128)(2,1)} %param.8) | copy-start | bytes 786436
  59.1 566.1 %all-to-all-start.1 = ((bf16[32,2,28672]{2,1,0:T(2,128)(2,1)}), bf16[32,2,28672]{2,1,0:T(2,128)(2,1)}, u32[]{:S(2)}, u32[]{:S(2)}) async-start(bf16[32,2,28672]{2,1,0:T(2,128)(2,1)} %reshape.64), calls=%async_computation.5 | async-start | bytes 7340032 | tf_op jit(solution)/shard_map/all_to_all | solution.py:43
  69.4 300.2 %reduce-scatter.9.cloned.1.call-start = ((), (), s32[]{:S(2)}) async-start(), calls=%async_computation.8 | async-start | bytes 1179648 | tf_op jit(solution)/shard_map/reduce_scatter | solution.py:19
  625.2 120.1 %all-to-all-start = ((bf16[32,2,28672]{2,1,0:T(2,128)(2,1)}), bf16[32,2,28672]{2,1,0:T(2,128)(2,1)}, u32[]{:S(2)}, u32[]{:S(2)}) async-start(bf16[32,2,28672]{2,1,0:T(2,128)(2,1)} %reshape.62), calls=%async_computation.4 | async-start | bytes 7340032 | tf_op jit(solution)/shard_map/all_to_all | solution.py:42
  663.4 233.5 %all-gather.2.cloned.1.call-start = ((), (), s32[]{:S(2)}) async-start(), calls=%async_computation.10 | async-start | bytes 15138816 | tf_op jit(solution)/shard_map/all_gather | solution.py:54
  794.1 6.0 copy-start
  794.1 6.0 copy-start.4
Sparse Core Ops, SparseCore 0:
  11.3 89.5 reduce-scatter.10
  105.3 90.5 reduce-scatter.4
  199.8 82.6 reduce-scatter.6
  286.8 82.7 reduce-scatter.8
  812.1 84.7 all-gather.1
where the time goes:
time: 926 us; the launch traced here: 917 us
  waiting for transfers between devices  409 us (44%)
  blocking collectives  189 us (20%)
  local copies, waits for them, and re-layouts  134 us (14%)
  other arithmetic  84.6 us (9%)
  starting transfers between devices  48.7 us (5%)
  matrix products  35.4 us (4%)
  between operations  16.3 us (2%)
    reduce_scatter x4, waiting for transfers between devices, body(): lax.psum_scatter(jnp.dot(batch_hidden, local_weight, preferred_element_ty...  296 us
    all_gather x4, blocking collectives, body(): lax.all_gather(grad_out, 'mp', axis=0, tiled=True)  168 us
    all_gather x1, waiting for transfers between devices, body(): every_cluster = lax.all_gather(merged, 'client', axis=1, tiled=True)  82.3 us
    unnamed x18, local copies, waits for them, and re-layouts  64.4 us
    unnamed x2, other arithmetic  47.4 us
    all_to_all x1, starting transfers between devices, body(): lax.all_to_all(a_weight[None], 'client', split_axis=1, concat_axis=0, til...  38.2 us
    all_to_all x1, waiting for transfers between devices, body(): lax.all_to_all(a_weight[None], 'client', split_axis=1, concat_axis=0, til...  30.2 us
    all_to_all x2, local copies, waits for them, and re-layouts, body(): lax.all_to_all(a_weight[None], 'client', split_axis=1, concat_axis=0, til...  29.5 us
  transfers between devices with their start and end apart: 7, of which 6 were waited for; matrix products, arithmetic and copies ran while one was open for 19% of the time, Pallas kernels for 0%

commit v1 on v0

--- a/solution.py
+++ b/solution.py
@@ -39,7 +39,15 @@
     mean_fisher = total_fisher / (FFW * D)
     a_weight = (fisher / (mean_fisher + EPS) + FLOOR).astype(jnp.bfloat16)
     got_a, got_w = (
-        lax.all_to_all(a_weight[None], "client", split_axis=1, concat_axis=0, tiled=True),
+        jnp.concatenate(
+            lax.all_to_all(
+                jnp.stack(jnp.split(a_weight[None], lax.axis_size("client"), axis=1)),
+                "client",
+                0,
+                0,
+            ),
+            axis=0,
+        ),
         lax.all_to_all(local_weight[None], "client", split_axis=1, concat_axis=0, tiled=True),
     )
     member_table = (assign[:, 0][:, None] == jnp.arange(CLUSTERS)[None, :]).astype(jnp.float32)

time: 926 us -> 849 us (0.917)
  local copies, waits for them, and re-layouts: 134 us -> 79.9 us
  other arithmetic: 84.6 us -> 59.3 us
  waiting for transfers between devices: 409 us -> 420 us
    all_to_all x2 -> x0, local copies, waits for them, and re-layouts: 29.5 us -> none  [body(): lax.all_to_all(a_weight[None], 'client', split_axis=1, concat_axis=0, til...]
    unnamed x2 -> x1, other arithmetic: 47.4 us -> 23.7 us
    broadcast_in_dim x1 -> x0, local copies, waits for them, and re-layouts: 18.1 us -> none  [body(): a_weight[None]]
    all_to_all x1, waiting for transfers between devices: 30.2 us -> 41.6 us  [body(): lax.all_to_all(jnp.stack(jnp.split(a_weight[None], lax.axis_size('client'...]
    unnamed x18 -> x45, local copies, waits for them, and re-layouts: 64.4 us -> 57.1 us
  transfers between devices with their start and end apart: 7 -> 7, of which waited for: 6 -> 6; matrix products, arithmetic and copies ran while one was open for 19% -> 16% of each run, Pallas kernels for 0% -> 0%
where the time goes in v1:
time: 849 us; the launch traced here: 847 us
  waiting for transfers between devices  420 us (49%)
  blocking collectives  190 us (22%)
  local copies, waits for them, and re-layouts  79.9 us (9%)
  other arithmetic  59.3 us (7%)
  starting transfers between devices  45.2 us (5%)
  matrix products  37.6 us (4%)
  between operations  15.8 us (2%)
    reduce_scatter x4, waiting for transfers between devices, body(): lax.psum_scatter(jnp.dot(batch_hidden, local_weight, preferred_element_ty...  296 us
    all_gather x4, blocking collectives, body(): lax.all_gather(grad_out, 'mp', axis=0, tiled=True)  166 us
    all_gather x1, waiting for transfers between devices, body(): every_cluster = lax.all_gather(merged, 'client', axis=1, tiled=True)  82.4 us
    unnamed x45, local copies, waits for them, and re-layouts  57.1 us
    all_to_all x1, waiting for transfers between devices, body(): lax.all_to_all(jnp.stack(jnp.split(a_weight[None], lax.axis_size('client'...  41.6 us
    all_to_all x1, starting transfers between devices, body(): lax.all_to_all(jnp.stack(jnp.split(a_weight[None], lax.axis_size('client'...  34.6 us
    convert_element_type x1, other arithmetic, body(): weighted = a_float * got_w.astype(jnp.float32)  24.4 us
    unnamed x1, other arithmetic  23.7 us
  transfers between devices with their start and end apart: 7, of which 6 were waited for; matrix products, arithmetic and copies ran while one was open for 16% of the time, Pallas kernels for 0%

profile of v1, /device:TPU:1, one launch (start us, length us, event | category | flops | bytes accessed | tf_op | source)
XLA Modules:
  0.0 847.5 jit_solution(8010446990004672633)
XLA Ops:
  6.5 3.9 fusion.2
  10.6 3.8 fusion.8
  14.4 3.8 fusion.6
  18.2 3.8 fusion.4
  22.0 7.8 copy.27
  30.4 23.7 %reduce.7 = bf16[896,2048]{1,0:T(8,128)(2,1)} reduce(bf16[896,1,2048]{2,1,0:T(2,128)(2,1)} %bitcast.200, bf16[]{:T(256)} %broadcast.40), dimensions={1}, to_apply=%bitcast.199.reduce_sub_computation | reduce | bytes 7340034
  54.1 8.7 %reshape.62 = bf16[32,2,28672]{2,1,0:T(2,128)(2,1)} reshape(bf16[896,2048]{1,0:T(8,128)(2,1)} %reduce.7) | data formatting | bytes 7340032
  62.9 10.4 %all-to-all-start.1 = ((bf16[32,2,28672]{2,1,0:T(2,128)(2,1)}), bf16[32,2,28672]{2,1,0:T(2,128)(2,1)}, u32[]{:S(2)}, u32[]{:S(2)}) async-start(bf16[32,2,28672]{2,1,0:T(2,128)(2,1)} %reshape.62), calls=%async_computation.5 | async-start | bytes 7340032 | tf_op jit(solution)/shard_map/all_to_all | solution.py:51
  73.3 27.4 %reduce-scatter.11.cloned.1.call-done = f32[16,2048]{1,0:T(8,128)} async-done(((f32[128,2048]{1,0:T(8,128)}), f32[16,2048]{1,0:T(8,128)}) %reduce-scatter.11.cloned.1.call-update) | async-done | bytes 131088 | tf_op jit(solution)/shard_map/reduce_scatter | solution.py:19
  100.7 95.2 %reduce-scatter.5.cloned.1.call-done = f32[16,2048]{1,0:T(8,128)} async-done(((f32[128,2048]{1,0:T(8,128)}), f32[16,2048]{1,0:T(8,128)}) %reduce-scatter.5.cloned.1.call-update) | async-done | bytes 131088 | tf_op jit(solution)/shard_map/reduce_scatter | solution.py:19
  195.8 86.6 %reduce-scatter.7.cloned.1.call-done = f32[16,2048]{1,0:T(8,128)} async-done(((f32[128,2048]{1,0:T(8,128)}), f32[16,2048]{1,0:T(8,128)}) %reduce-scatter.7.cloned.1.call-update) | async-done | bytes 131088 | tf_op jit(solution)/shard_map/reduce_scatter | solution.py:19
  282.4 86.9 %reduce-scatter.9.cloned.1.call-done = f32[16,2048]{1,0:T(8,128)} async-done(((f32[128,2048]{1,0:T(8,128)}), f32[16,2048]{1,0:T(8,128)}) %reduce-scatter.9.cloned.1.call-update) | async-done | bytes 131088 | tf_op jit(solution)/shard_map/reduce_scatter | solution.py:19
  369.3 1.2 fusion.71
  370.5 40.8 %all_gather.17 = bf16[128,2048]{1,0:T(8,128)(2,1)S(1)} all-gather(bf16[16,2048]{1,0:T(8,128)(2,1)S(1)} %get-tuple-element.12), channel_id=1, replica_groups=mesh['client'=32,'mp'=8] {'mp'}, dimensions={0}, use_global_device_ids=true | all-gather | bytes 589824 | tf_op jit(solution)/shard_map/all_gather | solution.py:33
  411.3 1.2 fusion.21
  412.4 43.6 %all_gather.16 = bf16[128,2048]{1,0:T(8,128)(2,1)S(1)} all-gather(bf16[16,2048]{1,0:T(8,128)(2,1)S(1)} %get-tuple-element.10), channel_id=1, replica_groups=mesh['client'=32,'mp'=8] {'mp'}, dimensions={0}, use_global_device_ids=true | all-gather | bytes 589824 | tf_op jit(solution)/shard_map/all_gather | solution.py:33
  456.0 1.2 fusion.24
  457.2 40.2 %all_gather.15 = bf16[128,2048]{1,0:T(8,128)(2,1)S(1)} all-gather(bf16[16,2048]{1,0:T(8,128)(2,1)S(1)} %get-tuple-element.11), channel_id=1, replica_groups=mesh['client'=32,'mp'=8] {'mp'}, dimensions={0}, use_global_device_ids=true | all-gather | bytes 589824 | tf_op jit(solution)/shard_map/all_gather | solution.py:33
  497.4 1.2 fusion.27
  498.5 41.6 %all_gather.18 = bf16[128,2048]{1,0:T(8,128)(2,1)S(1)} all-gather(bf16[16,2048]{1,0:T(8,128)(2,1)S(1)} %get-tuple-element.9), channel_id=1, replica_groups=mesh['client'=32,'mp'=8] {'mp'}, dimensions={0}, use_global_device_ids=true | all-gather | bytes 589824 | tf_op jit(solution)/shard_map/all_gather | solution.py:33
  540.1 5.0 fusion.83
  545.1 23.5 %psum.7 = f32[]{:T(128)} all-reduce(f32[]{:T(128)} %get-tuple-element.17), channel_id=1, replica_groups=mesh['client'=32,'mp'=8] {'mp'}, use_global_device_ids=true, to_apply=%region_9.10 | all-reduce | flops 1 | bytes 8 | tf_op jit(solution)/shard_map/psum | solution.py:38
  569.2 4.1 fusion.12
  573.3 0.7 fusion.69
  574.0 0.7 fusion.68
  574.7 0.7 fusion.67
  575.3 0.7 fusion.66
  576.6 0.7 fusion.64
  578.0 0.7 fusion.62
  579.3 0.7 fusion.60
  580.0 0.7 fusion.59
  580.6 0.7 fusion.58
  581.3 0.7 fusion.57
  582.0 0.7 fusion.56
  582.7 0.7 fusion.55
  583.3 0.7 fusion.54
  584.0 0.7 fusion.53
  584.7 0.7 fusion.52
  585.4 0.7 fusion.51
  586.0 0.7 fusion.50
  586.7 0.7 fusion.49
  587.4 0.7 fusion.48
  588.1 0.7 fusion.47
  588.7 0.7 fusion.46
  589.4 0.7 fusion.45
  590.1 0.7 fusion.44
  590.7 0.7 fusion.43
  591.4 0.7 fusion.42
  592.1 0.7 fusion.41
  592.8 0.7 fusion.40
  593.4 0.7 fusion.39
  594.1 0.7 fusion.38
  594.8 34.6 %all-to-all-start = ((bf16[32,1,28,2048]{3,2,1,0:T(8,128)(2,1)}), bf16[32,1,28,2048]{3,2,1,0:T(8,128)(2,1)}, u32[]{:S(2)}, u32[]{:S(2)}) async-start(bf16[32,1,28,2048]{3,2,1,0:T(8,128)(2,1)} %fusion.38), calls=%async_computation.4 | async-start | bytes 8388608 | tf_op jit(solution)/shard_map/all_to_all | solution.py:43
  629.5 19.3 %reshape.63 = bf16[896,1,2048]{2,1,0:T(2,128)(2,1)} reshape(bf16[32,2,28672]{2,1,0:T(2,128)(2,1)} %all-to-all-done.1) | data formatting | bytes 7340032
  648.8 24.4 %convert_reduce_fusion = f32[896,2048]{1,0:T(8,128)} fusion(bf16[896,1,2048]{2,1,0:T(2,128)(2,1)} %reshape.63), kind=kLoop, calls=%fused_computation.4 | loop fusion | flops 1835008 | bytes 11010048 | tf_op jit(solution)/shard_map/convert_element_type | solution.py:55
  673.2 8.0 reshape.59
  681.2 41.6 %all-to-all-done = bf16[32,1,28,2048]{3,2,1,0:T(8,128)(2,1)} async-done(((bf16[32,1,28,2048]{3,2,1,0:T(8,128)(2,1)}), bf16[32,1,28,2048]{3,2,1,0:T(8,128)(2,1)}, u32[]{:S(2)}, u32[]{:S(2)}) %all-to-all-start) | async-done | bytes 3670048 | tf_op jit(solution)/shard_map/all_to_all | solution.py:43
  722.7 6.2 fusion.10
  728.9 5.8 convert_multiply_fusion
  734.8 7.7 fusion.16
  742.5 0.6 constant_dynamic-slice_fusion.1
  745.1 82.4 %all-gather.2.cloned.1.call-done = bf16[4,896,2048]{2,0,1:T(4,128)(2,1)} async-done(((bf16[4,28,2048]{2,0,1:T(4,128)(2,1)}), bf16[4,896,2048]{2,0,1:T(4,128)(2,1)}) %all-gather.2.cloned.1.call-update) | async-done | bytes 14680080 | tf_op jit(solution)/shard_map/all_gather | solution.py:62
  827.5 9.3 %constant_dynamic-slice_fusion = bf16[1,896,2048]{2,0,1:T(2,128)(2,1)S(1)} fusion(bf16[4,896,2048]{2,0,1:T(4,128)(2,1)} %all-gather.2.cloned.1.call-done, s32[]{:T(128)S(6)} %select_n.42), kind=kLoop, calls=%fused_computation.126 | loop fusion | bytes 7340036 | tf_op jit(solution)/shard_map/jit(dynamic_index_in_dim)/dynamic_slice | solution.py:63
  836.8 4.1 copy.16
  (27 shorter events, 2.8 us)
Async XLA Ops:
  6.5 4.0 copy-start
  6.5 94.1 %reduce-scatter.11.cloned.1.call-start = ((), (), s32[]{:S(2)}) async-start(), calls=%async_computation.9 | async-start | bytes 1179648 | tf_op jit(solution)/shard_map/reduce_scatter | solution.py:19
  10.5 185.3 %reduce-scatter.5.cloned.1.call-start = ((), (), s32[]{:S(2)}) async-start(), calls=%async_computation.6 | async-start | bytes 1179648 | tf_op jit(solution)/shard_map/reduce_scatter | solution.py:19
  14.3 268.1 %reduce-scatter.7.cloned.1.call-start = ((), (), s32[]{:S(2)}) async-start(), calls=%async_computation.7 | async-start | bytes 1179648 | tf_op jit(solution)/shard_map/reduce_scatter | solution.py:19
  18.2 351.2 %reduce-scatter.9.cloned.1.call-start = ((), (), s32[]{:S(2)}) async-start(), calls=%async_computation.8 | async-start | bytes 1179648 | tf_op jit(solution)/shard_map/reduce_scatter | solution.py:19
  62.9 10.4 %copy-start.2 = (s32[1,4,16,2]{2,3,1,0:T(2,128)S(1)}, s32[1,4,16,2]{2,3,1,0:T(2,128)}, u32[]{:S(2)}) copy-start(s32[1,4,16,2]{2,3,1,0:T(2,128)} %param.10) | copy-start | bytes 1540
  62.9 10.4 %copy-start.4 = (f32[1,4,16]{2,1,0:T(4,128)S(1)}, f32[1,4,16]{2,1,0:T(4,128)}, u32[]{:S(2)}) copy-start(f32[1,4,16]{2,1,0:T(4,128)} %param.9) | copy-start | bytes 772
  62.9 306.5 %copy-start.1 = (bf16[1,4,16,2048]{3,2,1,0:T(8,128)(2,1)S(1)}, bf16[1,4,16,2048]{3,2,1,0:T(8,128)(2,1)}, u32[]{:S(2)}) copy-start(bf16[1,4,16,2048]{3,2,1,0:T(8,128)(2,1)} %param.8) | copy-start | bytes 786436
  62.9 531.9 %all-to-all-start.1 = ((bf16[32,2,28672]{2,1,0:T(2,128)(2,1)}), bf16[32,2,28672]{2,1,0:T(2,128)(2,1)}, u32[]{:S(2)}, u32[]{:S(2)}) async-start(bf16[32,2,28672]{2,1,0:T(2,128)(2,1)} %reshape.62), calls=%async_computation.5 | async-start | bytes 7340032 | tf_op jit(solution)/shard_map/all_to_all | solution.py:51
  594.8 128.0 %all-to-all-start = ((bf16[32,1,28,2048]{3,2,1,0:T(8,128)(2,1)}), bf16[32,1,28,2048]{3,2,1,0:T(8,128)(2,1)}, u32[]{:S(2)}, u32[]{:S(2)}) async-start(bf16[32,1,28,2048]{3,2,1,0:T(8,128)(2,1)} %fusion.38), calls=%async_computation.4 | async-start | bytes 8388608 | tf_op jit(solution)/shard_map/all_to_all | solution.py:43
  629.4 198.1 %all-gather.2.cloned.1.call-start = ((), (), s32[]{:S(2)}) async-start(), calls=%async_computation.10 | async-start | bytes 15138816 | tf_op jit(solution)/shard_map/all_gather | solution.py:62
  673.2 49.6 %copy-start.3 = (s32[32,1]{0,1:T(1,128)S(1)}, s32[32,1]{0,1:T(1,128)}, u32[]{:S(2)}) copy-start(s32[32,1]{0,1:T(1,128)} %param.11) | copy-start | bytes 388
Sparse Core Ops, SparseCore 0:
  11.3 89.3 reduce-scatter.10
  105.1 90.6 reduce-scatter.4
  199.8 82.5 reduce-scatter.6
  286.7 82.5 reduce-scatter.8
  742.6 84.7 all-gather.1
